TPU v7x, 32 devices: a whole 2x2x4 slice. The times are simulated.
32 devices in a mesh: expert: 8 (over z, x), opt: 4 (over y, core).
Axes of the slice: x: 2, y: 2, z: 4, core: 2. Of those that a mesh axis runs over, the one named last changes fastest.
Arguments:
- out_grad: bfloat16 [16384, 2048], P(('expert', 'opt')), may hold values from -6 to 6
- saved_input: bfloat16 [16384, 768], P(('expert', 'opt')), may hold values from -6 to 6
- route: int32 [16384, 1], P(('expert', 'opt')), may hold values from 0 to 31, as said below
- place_now: int32 [32], replicated, may hold values from 0 to 7, as said below
- place_next: int32 [32], replicated, may hold values from 0 to 7, as said below
- master: float32 [8, 1572864], P(None, ('expert', 'opt')), may hold values from -0.21875 to 0.21875
- moment_one: float32 [8, 1572864], P(None, ('expert', 'opt')), may hold values from -2 to 2
- moment_two: float32 [8, 1572864], P(None, ('expert', 'opt')), may hold values from 0.01 to 1
- fwd_input: bfloat16 [32768, 768], P(('expert', 'opt')), may hold values from -6 to 6
Outputs:
- input_grad: bfloat16 [16384, 768], P(('expert', 'opt'))
- new_master: float32 [8, 1572864], P(None, ('expert', 'opt'))
- new_moment_one: float32 [8, 1572864], P(None, ('expert', 'opt'))
- new_moment_two: float32 [8, 1572864], P(None, ('expert', 'opt'))
- fwd_output: bfloat16 [32768, 2048], P(('expert', 'opt'))
Inputs may be any that keep to these rules, and one draw needn't show every extreme that they name: `route`: among the 512 rows of one device, at most 32 go to one replica device; in every draw some replica device receives exactly 32 rows from every device. `place_now`: every one of the 8 experts holds at least one replica slot. `place_next`: every one of the 8 experts holds at least one replica slot.
All inputs are finite; a program needn't handle non-finite values.
Results may differ from a plain program's by a relative error of at most 0.005.
Values may be sent and summed in bfloat16 or wider, within the bound.
A program may use at most 128 MiB of HBM per device.

v0:
```python
import jax
import jax.numpy as jnp
from jax import lax
from jax.sharding import PartitionSpec as P

LOSS_SCALE = 64.0
BETA_ONE = 0.9
BETA_TWO = 0.95
LEARN_RATE = 0.002
DECAY = 0.1
EPSILON = 1e-08
STEP_COUNT = 20.0


def replica_weights(weights, placement, hidden_width, model_width):
    picked = jnp.take(weights.astype(jnp.bfloat16), placement, axis=0)
    arrived = lax.all_to_all(picked, ("expert", "opt"), split_axis=0, concat_axis=0, tiled=True)
    return arrived.reshape(hidden_width, model_width)


def per_device(
    out_grad, saved_input, route, place_now, place_next, master, moment_one, moment_two, fwd_input
):
    groups = lax.axis_size("expert")
    members = lax.axis_size("opt")
    device_count = groups * members
    rows_here = out_grad.shape[0]
    model_width = out_grad.shape[1]
    hidden_width = saved_input.shape[1]
    capacity = 2 * rows_here // device_count
    slot_count = device_count * capacity
    target = route[:, 0]
    matches = (target[:, None] == jnp.arange(device_count, dtype=jnp.int32)[None, :]).astype(
        jnp.int32
    )
    earlier = jnp.sum(jnp.cumsum(matches, axis=0) * matches, axis=1) - 1
    position = target * capacity + earlier
    hidden_send = jnp.zeros((slot_count, hidden_width), jnp.bfloat16).at[position].set(saved_input)
    grad_send = jnp.zeros((slot_count, model_width), jnp.bfloat16).at[position].set(out_grad)
    hidden_got, grad_got = (
        lax.all_to_all(hidden_send, ("expert", "opt"), split_axis=0, concat_axis=0, tiled=True),
        lax.all_to_all(grad_send, ("expert", "opt"), split_axis=0, concat_axis=0, tiled=True),
    )
    weight_now = replica_weights(master, place_now, hidden_width, model_width)
    input_part = lax.dot_general(
        grad_got, weight_now, (((1,), (1,)), ((), ())), preferred_element_type=jnp.float32
    ).astype(jnp.bfloat16)
    returned = lax.all_to_all(
        input_part, ("expert", "opt"), split_axis=0, concat_axis=0, tiled=True
    )
    input_grad = jnp.take(returned, position, axis=0)
    weight_part = (
        lax.dot_general(
            hidden_got, grad_got, (((0,), (0,)), ((), ())), preferred_element_type=jnp.float32
        )
        / LOSS_SCALE
    )
    pieces = weight_part.astype(jnp.bfloat16).reshape(device_count, -1)
    arrived = lax.all_to_all(pieces, ("expert", "opt"), split_axis=0, concat_axis=0, tiled=True)
    experts = master.shape[0]
    owners = (place_now[None, :] == jnp.arange(experts, dtype=jnp.int32)[:, None]).astype(
        jnp.float32
    )
    gradient = jnp.dot(
        owners,
        arrived.astype(jnp.float32),
        precision=lax.Precision.HIGHEST,
        preferred_element_type=jnp.float32,
    )
    new_moment_one = BETA_ONE * moment_one + (1.0 - BETA_ONE) * gradient
    new_moment_two = BETA_TWO * moment_two + (1.0 - BETA_TWO) * gradient * gradient
    first_hat = new_moment_one / (1.0 - BETA_ONE**STEP_COUNT)
    second_hat = new_moment_two / (1.0 - BETA_TWO**STEP_COUNT)
    new_master = master - LEARN_RATE * (
        first_hat / (jnp.sqrt(second_hat) + EPSILON) + DECAY * master
    )
    weight_next = replica_weights(new_master, place_next, hidden_width, model_width)
    fwd_output = jnp.dot(fwd_input, weight_next, preferred_element_type=jnp.float32).astype(
        jnp.bfloat16
    )
    return (input_grad, new_master, new_moment_one, new_moment_two, fwd_output)


def solution(mesh):
    return jax.shard_map(
        per_device,
        mesh=mesh,
        in_specs=(
            P(("expert", "opt"), None),
            P(("expert", "opt"), None),
            P(("expert", "opt"), None),
            P(),
            P(),
            P(None, ("expert", "opt")),
            P(None, ("expert", "opt")),
            P(None, ("expert", "opt")),
            P(("expert", "opt"), None),
        ),
        out_specs=(
            P(("expert", "opt"), None),
            P(None, ("expert", "opt")),
            P(None, ("expert", "opt")),
            P(None, ("expert", "opt")),
            P(("expert", "opt"), None),
        ),
        check_vma=False,
    )
```

profile of v0, /device:TPU:0, one launch (start us, length us, event | category | flops | bytes accessed | tf_op | source)
XLA Modules:
  0.0 541.8 jit_solution(3865157308173567724)
XLA Ops:
  0.6 0.0 copy-start
  0.6 0.8 fusion.11
  1.5 1.2 reduce-window.6
  2.6 0.2 slice_reduce_fusion
  2.9 0.8 fusion.10
  3.7 0.7 and_reduce_fusion
  4.4 4.4 scatter_custom_fusion.1
  8.8 7.3 %all-to-all-start.3 = ((bf16[32,32,768]{2,1,0:T(8,128)(2,1)}), bf16[32,32,768]{2,1,0:T(8,128)(2,1)S(1)}, u32[]{:S(2)}, u32[]{:S(2)}) async-start(bf16[32,32,768]{2,1,0:T(8,128)(2,1)} %bitcast.10), calls=%async_computation.3 | async-start | bytes 3145728 | tf_op jit(solution)/shard_map/all_to_all | solution.py:41
  16.1 7.3 %scatter_custom_fusion = bf16[1024,2048]{1,0:T(8,128)(2,1)} fusion(s32[512]{0:T(512)S(1)} %bitcast.52, bf16[512,2048]{1,0:T(8,128)(2,1)} %param.11, bf16[]{:T(256)} %constant.23.clone.1), kind=kCustom, calls=%fused_computation.14 | custom fusion | bytes 4194816 | tf_op jit(solution)/shard_map/scatter | solution.py:39
  23.4 30.1 %all-to-all-done.3 = bf16[32,32,768]{2,1,0:T(8,128)(2,1)S(1)} async-done(((bf16[32,32,768]{2,1,0:T(8,128)(2,1)}), bf16[32,32,768]{2,1,0:T(8,128)(2,1)S(1)}, u32[]{:S(2)}, u32[]{:S(2)}) %all-to-all-start.3) | async-done | bytes 1572896 | tf_op jit(solution)/shard_map/all_to_all | solution.py:41
  53.5 97.4 %all_to_all.64 = bf16[32,32,2048]{2,1,0:T(8,128)(2,1)S(1)} all-to-all(bf16[32,32,2048]{2,1,0:T(8,128)(2,1)} %bitcast.46), channel_id=1, replica_groups=mesh['expert'=8,'opt'=4] {'expert','opt'}, dimensions={0} | all-to-all | bytes 8388608 | tf_op jit(solution)/shard_map/all_to_all | solution.py:42
  150.9 0.0 copy-start.1
  150.9 2.0 copy-done.1
  152.9 4.9 fusion
  157.9 12.4 %all_to_all.57 = bf16[32,1,49152]{2,1,0:T(2,128)(2,1)} reshape(bf16[768,2048]{1,0:T(8,128)(2,1)} %fusion) | data formatting | bytes 6291456 | tf_op jit(solution)/shard_map/all_to_all | solution.py:59
  170.2 0.5 broadcast.77
  170.7 20.7 %reduce.6 = bf16[32,49152]{1,0:T(8,128)(2,1)} reduce(bf16[32,1,49152]{2,1,0:T(2,128)(2,1)} %all_to_all.57, bf16[]{:T(256)} %broadcast.77), dimensions={1}, to_apply=%all_to_all.57.reduce_sub_computation | reduce | bytes 6291458 | tf_op jit(solution)/shard_map/all_to_all | solution.py:59
  191.4 5.4 reshape.128
  196.8 0.0 copy-start.2
  196.8 0.0 copy-start.3
  196.8 3.8 all-to-all-start.4
  200.6 0.0 copy-done.2
  200.7 0.0 copy-done.3
  200.7 71.5 %all-to-all-done.4 = bf16[32,2,24576]{2,1,0:T(2,128)(2,1)} async-done(((bf16[32,2,24576]{2,1,0:T(2,128)(2,1)}), bf16[32,2,24576]{2,1,0:T(2,128)(2,1)}, u32[]{:S(2)}, u32[]{:S(2)}) %all-to-all-start.4) | async-done | bytes 3145760 | tf_op jit(solution)/shard_map/all_to_all | solution.py:59
  272.2 18.9 %reshape.129 = bf16[32,1,49152]{2,1,0:T(2,128)(2,1)} reshape(bf16[32,2,24576]{2,1,0:T(2,128)(2,1)} %all-to-all-done.4) | data formatting | bytes 6291456
  291.1 11.2 %fusion.13 = (bf16[8,49152]{1,0:T(8,128)(2,1)S(1)}, f32[8,49152]{1,0:T(8,128)}, f32[8,49152]{1,0:T(8,128)}, f32[8,49152]{1,0:T(8,128)}, bf16[8,49152]{1,0:T(8,128)(2,1)S(1)}) fusion(f32[8,49152]{1,0:T(8,128)} %param.16, f32[8,49152]{1,0:T(8,128)} %param.17, f32[8,49152]{1,0:T(8,128)} %param.18, bf16[32,1,49152]{2,1,0:T(2,128)(2,1)} %reshape.129, ...), kind=kOutput, calls=%fused_computation.43 | convolution fusion | flops 31850752 | bytes 14155904 | tf_op jit(solution)/shard_map/dot_general | solution.py:64
  302.3 4.3 gather_fusion.1
  306.6 3.9 select_bitcast_fusion.1
  310.5 5.7 %reduce.7 = bf16[32,49152]{1,0:T(8,128)(2,1)} reduce(bf16[32,1,49152]{2,0,1:T(8,128)(2,1)} %select_bitcast_fusion.1, bf16[]{:T(256)} %broadcast.77), dimensions={1}, to_apply=%copy.23.reduce_sub_computation | reduce | bytes 6291458 | tf_op jit(solution)/shard_map/all_to_all | solution.py:17
  316.3 5.4 reshape.126
  321.7 4.9 all-to-all-start.1
  326.6 4.3 gather_fusion.2
  330.9 4.0 select_bitcast_fusion
  334.8 5.7 %reduce.8 = bf16[32,49152]{1,0:T(8,128)(2,1)} reduce(bf16[32,1,49152]{2,0,1:T(8,128)(2,1)} %select_bitcast_fusion, bf16[]{:T(256)} %broadcast.77), dimensions={1}, to_apply=%copy.25.reduce_sub_computation | reduce | bytes 6291458 | tf_op jit(solution)/shard_map/all_to_all | solution.py:17
  340.6 5.5 %reshape.130 = bf16[32,2,24576]{2,1,0:T(2,128)(2,1)} reshape(bf16[32,49152]{1,0:T(8,128)(2,1)} %reduce.8) | data formatting | bytes 6291456
  346.0 52.1 %all-to-all-done.1 = bf16[32,2,24576]{2,1,0:T(2,128)(2,1)} async-done(((bf16[32,2,24576]{2,1,0:T(2,128)(2,1)}), bf16[32,2,24576]{2,1,0:T(2,128)(2,1)}, u32[]{:S(2)}, u32[]{:S(2)}) %all-to-all-start.1) | async-done | bytes 3145760 | tf_op jit(solution)/shard_map/all_to_all | solution.py:17
  398.1 4.8 all-to-all-start.5
  402.9 18.9 %reshape.127 = bf16[32,1,49152]{2,1,0:T(2,128)(2,1)} reshape(bf16[32,2,24576]{2,1,0:T(2,128)(2,1)} %all-to-all-done.1) | data formatting | bytes 6291456
  421.8 20.0 %reduce.2 = bf16[32,49152]{1,0:T(8,128)(2,1)} reduce(bf16[32,1,49152]{2,1,0:T(2,128)(2,1)} %reshape.127, bf16[]{:T(256)} %constant.64), dimensions={1}, to_apply=%all_to_all.46.reduce_sub_computation | reduce | bytes 6291458 | tf_op jit(solution)/shard_map/all_to_all | solution.py:17
  441.8 4.8 reshape.69
  446.6 7.8 %convolution_convert_fusion = bf16[1024,768]{1,0:T(8,128)(2,1)} fusion(bf16[1024,2048]{1,0:T(8,128)(2,1)} %bitcast.47, bf16[768,2048]{1,0:T(8,128)(2,1)} %reshape.69), kind=kOutput, calls=%fused_computation.16 | convolution fusion | flops 3222011904 | bytes 8912896 | tf_op jit(solution)/shard_map/dot_general | solution.py:45
  454.4 20.1 %all-to-all-done.5 = bf16[32,2,24576]{2,1,0:T(2,128)(2,1)} async-done(((bf16[32,2,24576]{2,1,0:T(2,128)(2,1)}), bf16[32,2,24576]{2,1,0:T(2,128)(2,1)}, u32[]{:S(2)}, u32[]{:S(2)}) %all-to-all-start.5) | async-done | bytes 3145760 | tf_op jit(solution)/shard_map/all_to_all | solution.py:17
  474.5 4.8 all-to-all-start.2
  479.3 18.9 %reshape.131 = bf16[32,1,49152]{2,1,0:T(2,128)(2,1)} reshape(bf16[32,2,24576]{2,1,0:T(2,128)(2,1)} %all-to-all-done.5) | data formatting | bytes 6291456
  498.2 20.0 %reduce.3 = bf16[32,49152]{1,0:T(8,128)(2,1)} reduce(bf16[32,1,49152]{2,1,0:T(2,128)(2,1)} %reshape.131, bf16[]{:T(256)} %constant.64), dimensions={1}, to_apply=%all_to_all.56.reduce_sub_computation | reduce | bytes 6291458 | tf_op jit(solution)/shard_map/all_to_all | solution.py:17
  518.2 4.8 reshape.70
  523.1 0.0 copy-done
  523.1 7.0 %convert_bitcast_fusion = bf16[1024,2048]{0,1:T(8,128)(2,1)} fusion(bf16[768,2048]{1,0:T(8,128)(2,1)} %reshape.70, bf16[1024,768]{1,0:T(8,128)(2,1)S(1)} %copy-done), kind=kOutput, calls=%fused_computation.7 | convolution fusion | flops 3223322624 | bytes 8912896 | tf_op jit(solution)/shard_map/dot_general | solution.py:78
  530.1 6.4 %copy.26 = bf16[1024,2048]{1,0:T(8,128)(2,1)} copy(bf16[1024,2048]{0,1:T(8,128)(2,1)} %convert_bitcast_fusion) | data formatting | bytes 8388608
  536.5 0.0 all-to-all-done.2
  536.5 2.7 gather_fusion
  539.2 2.2 broadcast_select_fusion
  (10 shorter events, 0.1 us)
Async XLA Ops:
  0.6 522.4 %copy-start = (bf16[1024,768]{1,0:T(8,128)(2,1)S(1)}, bf16[1024,768]{1,0:T(8,128)(2,1)}, u32[]{:S(2)}) copy-start(bf16[1024,768]{1,0:T(8,128)(2,1)} %param.19) | copy-start | bytes 4718596
  8.8 44.8 %all-to-all-start.3 = ((bf16[32,32,768]{2,1,0:T(8,128)(2,1)}), bf16[32,32,768]{2,1,0:T(8,128)(2,1)S(1)}, u32[]{:S(2)}, u32[]{:S(2)}) async-start(bf16[32,32,768]{2,1,0:T(8,128)(2,1)} %bitcast.10), calls=%async_computation.3 | async-start | bytes 3145728 | tf_op jit(solution)/shard_map/all_to_all | solution.py:41
  150.9 2.0 copy-start.1
  196.8 3.8 copy-start.2
  196.8 3.8 copy-start.3
  196.8 75.4 %all-to-all-start.4 = ((bf16[32,2,24576]{2,1,0:T(2,128)(2,1)}), bf16[32,2,24576]{2,1,0:T(2,128)(2,1)}, u32[]{:S(2)}, u32[]{:S(2)}) async-start(bf16[32,2,24576]{2,1,0:T(2,128)(2,1)} %reshape.128), calls=%async_computation.4 | async-start | bytes 6291456 | tf_op jit(solution)/shard_map/all_to_all | solution.py:59
  321.7 76.5 %all-to-all-start.1 = ((bf16[32,2,24576]{2,1,0:T(2,128)(2,1)}), bf16[32,2,24576]{2,1,0:T(2,128)(2,1)}, u32[]{:S(2)}, u32[]{:S(2)}) async-start(bf16[32,2,24576]{2,1,0:T(2,128)(2,1)} %reshape.126), calls=%async_computation.1 | async-start | bytes 6291456 | tf_op jit(solution)/shard_map/all_to_all | solution.py:17
  398.1 76.4 %all-to-all-start.5 = ((bf16[32,2,24576]{2,1,0:T(2,128)(2,1)}), bf16[32,2,24576]{2,1,0:T(2,128)(2,1)}, u32[]{:S(2)}, u32[]{:S(2)}) async-start(bf16[32,2,24576]{2,1,0:T(2,128)(2,1)} %reshape.130), calls=%async_computation.5 | async-start | bytes 6291456 | tf_op jit(solution)/shard_map/all_to_all | solution.py:17
  474.5 62.0 %all-to-all-start.2 = ((bf16[32,32,768]{2,1,0:T(8,128)(2,1)}), bf16[32,32,768]{2,1,0:T(8,128)(2,1)S(1)}, u32[]{:S(2)}, u32[]{:S(2)}) async-start(bf16[32,32,768]{2,1,0:T(8,128)(2,1)} %bitcast.48), calls=%async_computation.2 | async-start | bytes 3145728 | tf_op jit(solution)/shard_map/all_to_all | solution.py:48
where the time goes:
time: 552 us; the launch traced here: 542 us
  waiting for transfers between devices  174 us (32%)
  local copies, waits for them, and re-layouts  127 us (23%)
  blocking collectives  97.4 us (18%)
  other arithmetic  85.7 us (16%)
  matrix products  30.9 us (6%)
  starting transfers between devices  25.6 us (5%)
    all_to_all x1, blocking collectives, per_device(): lax.all_to_all(grad_send, ('expert', 'opt'), split_axis=0, concat_axis=0,...  97.4 us
    unnamed x15, local copies, waits for them, and re-layouts  81.4 us
    all_to_all x2, waiting for transfers between devices, replica_weights(): lax.all_to_all(picked, ('expert', 'opt'), split_axis=0, concat_axis=0, ti...  72.2 us
    all_to_all x1, waiting for transfers between devices, per_device(): lax.all_to_all(pieces, ('expert', 'opt'), split_axis=0, concat_axis=0, ti...  71.5 us
    all_to_all x6, other arithmetic, replica_weights(): lax.all_to_all(picked, ('expert', 'opt'), split_axis=0, concat_axis=0, ti...  59.3 us
    all_to_all x1, waiting for transfers between devices, per_device(): lax.all_to_all(hidden_send, ('expert', 'opt'), split_axis=0, concat_axis=...  30.1 us
    all_to_all x1, other arithmetic, per_device(): lax.all_to_all(pieces, ('expert', 'opt'), split_axis=0, concat_axis=0, ti...  20.7 us
    all_to_all x2, local copies, waits for them, and re-layouts, per_device(): lax.all_to_all(pieces, ('expert', 'opt'), split_axis=0, concat_axis=0, ti...  12.9 us
  transfers between devices with their start and end apart: 5, of which 4 were waited for; matrix products, arithmetic and copies ran while one was open for 25% of the time, Pallas kernels for 0%

commit v1 on v0

--- a/solution.py
+++ b/solution.py
@@ -2,6 +2,8 @@
 import jax.numpy as jnp
 from jax import lax
 from jax.sharding import PartitionSpec as P
+from jax.experimental import pallas as pl
+from jax.experimental.pallas import tpu as pltpu
 
 LOSS_SCALE = 64.0
 BETA_ONE = 0.9
@@ -10,6 +12,8 @@
 DECAY = 0.1
 EPSILON = 1e-08
 STEP_COUNT = 20.0
+GATHER_BYTES = 32 * 1024 * 1024
+AXES = ("expert", "opt")
 
 
 def replica_weights(weights, placement, hidden_width, model_width):
@@ -81,9 +85,127 @@
     return (input_grad, new_master, new_moment_one, new_moment_two, fwd_output)
 
 
+def rows_kernel(master_ref, rows_ref):
+    experts = master_ref.shape[0]
+    width = rows_ref.shape[1]
+    for part in range(rows_ref.shape[0] // experts):
+        rows_ref[part * experts : (part + 1) * experts, :] = master_ref[
+            :, part * width : (part + 1) * width
+        ].astype(rows_ref.dtype)
+
+
+def expert_rows(master, model_width, per_step):
+    experts, flat = master.shape
+    steps = flat // model_width // per_step
+    return pl.pallas_call(
+        rows_kernel,
+        grid=(steps,),
+        in_specs=[pl.BlockSpec((experts, per_step * model_width), lambda i: (0, i))],
+        out_specs=pl.BlockSpec((per_step * experts, model_width), lambda i: (i, 0)),
+        out_shape=jax.ShapeDtypeStruct((flat // model_width * experts, model_width), jnp.bfloat16),
+    )(master)
+
+
+def adamw_kernel(grad_ref, master_ref, one_ref, two_ref, master_out, one_out, two_out, rows_out):
+    experts = master_ref.shape[0]
+    width = grad_ref.shape[1]
+    for part in range(grad_ref.shape[0] // experts):
+        rows = slice(part * experts, (part + 1) * experts)
+        columns = slice(part * width, (part + 1) * width)
+        gradient = grad_ref[rows, :].astype(jnp.float32)
+        new_one = BETA_ONE * one_ref[:, columns] + (1.0 - BETA_ONE) * gradient
+        new_two = BETA_TWO * two_ref[:, columns] + (1.0 - BETA_TWO) * gradient * gradient
+        first_hat = new_one / (1.0 - BETA_ONE**STEP_COUNT)
+        second_hat = new_two / (1.0 - BETA_TWO**STEP_COUNT)
+        master = master_ref[:, columns]
+        new_master = master - LEARN_RATE * (
+            first_hat / (jnp.sqrt(second_hat) + EPSILON) + DECAY * master
+        )
+        one_out[:, columns] = new_one
+        two_out[:, columns] = new_two
+        master_out[:, columns] = new_master
+        rows_out[rows, :] = new_master.astype(rows_out.dtype)
+
+
+def adamw(grad_rows, master, moment_one, moment_two, per_step):
+    experts, flat = master.shape
+    width = grad_rows.shape[1]
+    steps = flat // width // per_step
+    wide = pl.BlockSpec((experts, per_step * width), lambda i: (0, i))
+    tall = pl.BlockSpec((per_step * experts, width), lambda i: (i, 0))
+    state = jax.ShapeDtypeStruct(master.shape, jnp.float32)
+    return pl.pallas_call(
+        adamw_kernel,
+        grid=(steps,),
+        in_specs=[tall, wide, wide, wide],
+        out_specs=[wide, wide, wide, tall],
+        out_shape=[state, state, state, jax.ShapeDtypeStruct(grad_rows.shape, jnp.bfloat16)],
+    )(grad_rows, master, moment_one, moment_two)
+
+
+def gathered_device(
+    out_grad, saved_input, route, place_now, place_next, master, moment_one, moment_two, fwd_input
+):
+    device_count = lax.axis_size("expert") * lax.axis_size("opt")
+    model_width = out_grad.shape[1]
+    hidden_width = saved_input.shape[1]
+    rows_here = out_grad.shape[0]
+    experts = master.shape[0]
+    owned = hidden_width // device_count
+    per_step = 4 if owned % 4 == 0 else 2
+    weight_rows = lax.all_gather(
+        expert_rows(master, model_width, per_step), AXES, axis=0, tiled=True
+    )
+    replicas = jnp.arange(device_count, dtype=jnp.int32)
+    expert_of = jnp.sum(
+        jnp.where(route[:, 0][None, :] == replicas[:, None], place_now[:, None], 0), axis=0
+    )
+    expert_ids = jnp.arange(experts, dtype=jnp.int32)
+    mine = expert_of[None, :] == expert_ids[:, None]
+    spread = jnp.where(
+        mine[None, :, :], saved_input.T[:, None, :], jnp.zeros((), jnp.bfloat16)
+    ).reshape(hidden_width * experts, rows_here)
+    partial = (
+        jnp.dot(spread, out_grad, preferred_element_type=jnp.float32) / LOSS_SCALE
+    ).astype(jnp.bfloat16)
+    grad_rows = lax.psum_scatter(partial, AXES, scatter_dimension=0, tiled=True)
+    every = lax.dot_general(
+        weight_rows, out_grad, (((1,), (1,)), ((), ())), preferred_element_type=jnp.float32
+    ).reshape(hidden_width, experts, rows_here)
+    input_grad = jnp.sum(jnp.where(mine[None, :, :], every, 0.0), axis=1).astype(jnp.bfloat16).T
+    new_master, new_one, new_two, next_rows = adamw(
+        grad_rows, master, moment_one, moment_two, per_step
+    )
+    row_ids = jnp.arange(owned, dtype=jnp.int32)
+    chosen = (place_next[:, None] == expert_ids[None, :])[:, None, None, :] & (
+        row_ids[:, None] == row_ids[None, :]
+    )[None, :, :, None]
+    picked = jnp.dot(
+        chosen.reshape(device_count * owned, owned * experts).astype(jnp.bfloat16),
+        next_rows,
+        preferred_element_type=jnp.float32,
+    ).astype(jnp.bfloat16)
+    weight_next = lax.all_to_all(
+        picked.reshape(device_count, owned, model_width), AXES, split_axis=0, concat_axis=0, tiled=True
+    ).reshape(hidden_width, model_width)
+    fwd_output = jnp.dot(fwd_input, weight_next, preferred_element_type=jnp.float32).astype(
+        jnp.bfloat16
+    )
+    return (input_grad, new_master, new_one, new_two, fwd_output)
+
+
+def one_device(*arguments):
+    master = arguments[5]
+    devices = lax.axis_size("expert") * lax.axis_size("opt")
+    gathered = 2 * master.shape[0] * master.shape[1] * devices
+    if gathered <= GATHER_BYTES:
+        return gathered_device(*arguments)
+    return per_device(*arguments)
+
+
 def solution(mesh):
     return jax.shard_map(
-        per_device,
+        one_device,
         mesh=mesh,
         in_specs=(
             P(("expert", "opt"), None),

time: 552 us -> 512 us (0.928); the launches traced: 542 us -> 511 us
  waiting for transfers between devices: 174 us -> 303 us
  local copies, waits for them, and re-layouts: 127 us -> 11 us
  other arithmetic: 85.7 us -> 1.47 us
  blocking collectives: 97.4 us -> 125 us
  starting transfers between devices: 25.6 us -> 0.08 us
  matrix products: 30.9 us -> 45.6 us
  between operations: 1.21 us -> 14.1 us
  Pallas kernels: 0 us -> 10.8 us
    reduce_scatter x0 -> x1, waiting for transfers between devices: none -> 239 us  [gathered_device(): grad_rows = lax.psum_scatter(partial, AXES, scatter_dimension=0, tiled=True)]
    all_to_all x5 -> x0, waiting for transfers between devices: 174 us -> none  [the longest x2 72.2 us: replica_weights(): lax.all_to_all(picked, ('expert', 'opt'), split_axis=0, concat_axis=0, ti...]
    all_to_all x7 -> x0, other arithmetic: 80 us -> none  [the longest x6 59.3 us: replica_weights(): lax.all_to_all(picked, ('expert', 'opt'), split_axis=0, concat_axis=0, ti...]
    unnamed x15 -> x8, local copies, waits for them, and re-layouts: 81.4 us -> 7.61 us
    all_gather x0 -> x1, waiting for transfers between devices: none -> 63.9 us  [gathered_device(): lax.all_gather(expert_rows(master, model_width, per_step), AXES, axis=0,...]
    all_to_all x1, blocking collectives: 97.4 us -> 125 us  [gathered_device(): lax.all_to_all(picked.reshape(device_count, owned, model_width), AXES, sp...]
    all_to_all x5 -> x0, starting transfers between devices: 25.6 us -> none  [the longest x2 9.64 us: replica_weights(): lax.all_to_all(picked, ('expert', 'opt'), split_axis=0, concat_axis=0, ti...]
    dot_general x4, matrix products: 30.9 us -> 45.6 us  [the longest x1 21.5 us: gathered_device(): lax.dot_general(weight_rows, out_grad, (((1,), (1,)), ((), ())), preferre...]
  transfers between devices with their start and end apart: 5 -> 2, of which waited for: 4 -> 2; matrix products, arithmetic and copies ran while one was open for 25% -> 3% of each run, Pallas kernels for 0% -> 2%
where the time goes in v1:
time: 512 us; the launch traced here: 511 us
  waiting for transfers between devices  303 us (59%)
  blocking collectives  125 us (24%)
  matrix products  45.6 us (9%)
  between operations  14.1 us (3%)
  local copies, waits for them, and re-layouts  11 us (2%)
  Pallas kernels  10.8 us (2%)
    reduce_scatter x1, waiting for transfers between devices, gathered_device(): grad_rows = lax.psum_scatter(partial, AXES, scatter_dimension=0, tiled=True)  239 us
    all_to_all x1, blocking collectives, gathered_device(): lax.all_to_all(picked.reshape(device_count, owned, model_width), AXES, sp...  125 us
    all_gather x1, waiting for transfers between devices, gathered_device(): lax.all_gather(expert_rows(master, model_width, per_step), AXES, axis=0,...  63.9 us
    dot_general x1, matrix products, gathered_device(): lax.dot_general(weight_rows, out_grad, (((1,), (1,)), ((), ())), preferre...  21.5 us
    dot_general x1, matrix products, gathered_device(): jnp.dot(spread, out_grad, preferred_element_type=jnp.float32) / LOSS_SCALE  16.9 us
  transfers between devices with their start and end apart: 2, of which 2 were waited for; matrix products, arithmetic and copies ran while one was open for 3% of the time, Pallas kernels for 2%

profile of v1, /device:TPU:0, one launch (start us, length us, event | category | flops | bytes accessed | tf_op | source)
XLA Modules:
  0.0 511.3 jit_solution(9009250370056646001)
XLA Ops:
  7.2 0.0 copy-start
  7.2 0.0 reduce-scatter.2.cloned.1.call-start
  7.2 0.9 select_reduce_fusion
  8.2 1.4 copy.21
  9.6 0.0 copy-done
  9.6 16.9 %multiply_convert_fusion = bf16[6144,2048]{1,0:T(8,128)(2,1)} fusion(bf16[512,2048]{1,0:T(8,128)(2,1)S(1)} %copy-done, pred[8,512]{1,0:T(8,128)(4,1)S(1)} %iota_compare_fusion.1, bf16[768,512]{1,0:T(8,128)(2,1)S(1)} %copy.21), kind=kOutput, calls=%fused_computation | convolution fusion | flops 12913213440 | bytes 28053504 | tf_op jit(solution)/shard_map/dot_general | solution.py:169
  26.4 0.0 reduce-scatter.2.cloned.1.call-update
  26.5 0.0 copy-start.2
  26.5 0.0 all-gather.2.cloned.1.call-start
  26.5 4.3 shard_map.128
  30.9 0.0 all-gather.2.cloned.1.call-update
  30.9 0.0 copy-done.2
  30.9 0.5 broadcast_and_fusion
  31.5 2.0 and.20
  33.4 239.0 %reduce-scatter.2.cloned.1.call-done.grad_ref = bf16[192,2048]{1,0:T(8,128)(2,1)} async-done(((bf16[6144,2048]{1,0:T(8,128)(2,1)}), bf16[192,2048]{1,0:T(8,128)(2,1)}) %reduce-scatter.2.cloned.1.call-update) | async-done | bytes 786448 | tf_op jit(solution)/shard_map/reduce_scatter | solution.py:171
  272.4 6.5 %shard_map.129 = (f32[8,49152]{1,0:T(8,128)}, f32[8,49152]{1,0:T(8,128)}, f32[8,49152]{1,0:T(8,128)}, bf16[192,2048]{1,0:T(8,128)(2,1)}) custom-call(bf16[192,2048]{1,0:T(8,128)(2,1)} %reduce-scatter.2.cloned.1.call-done.grad_ref, f32[8,49152]{1,0:T(8,128)} %master_ref.3, f32[8,49152]{1,0:T(8,128)} %one_ref.1, f32[8,49152]{1,0:T(8,128)} %two_ref.1), custom_call_target="tpu_custom_call" | custom-call | tf_op jit(solution)/shard_map/pallas_call | solution.py:137
  278.9 2.2 convolution_convert_fusion
  281.0 0.0 copy-start.1
  281.1 125.3 %all_to_all.5 = bf16[32,24,2048]{2,1,0:T(8,128)(2,1)S(1)} all-to-all(bf16[32,24,2048]{2,1,0:T(8,128)(2,1)S(1)} %bitcast.27), channel_id=1, replica_groups=mesh['expert'=8,'opt'=4] {'expert','opt'}, dimensions={0} | all-to-all | bytes 6291456 | tf_op jit(solution)/shard_map/all_to_all | solution.py:188
  406.4 0.0 copy-done.1
  406.4 5.1 convert_bitcast_fusion
  411.4 6.4 %copy.23 = bf16[1024,2048]{1,0:T(8,128)(2,1)} copy(bf16[1024,2048]{0,1:T(8,128)(2,1)} %convert_bitcast_fusion) | data formatting | bytes 8388608
  417.8 63.9 %all-gather.2.cloned.1.call-done = bf16[6144,2048]{1,0:T(8,128)(2,1)} async-done(((bf16[192,2048]{1,0:T(8,128)(2,1)}), bf16[6144,2048]{1,0:T(8,128)(2,1)}) %all-gather.2.cloned.1.call-update) | async-done | bytes 25165840 | tf_op jit(solution)/shard_map/all_gather | solution.py:156
  481.8 21.5 %fusion = bf16[768,512]{1,0:T(8,128)(2,1)S(1)} fusion(pred[8,512]{1,0:T(8,128)(4,1)S(1)} %iota_compare_fusion.1, bf16[6144,2048]{1,0:T(8,128)(2,1)} %all-gather.2.cloned.1.call-done, bf16[512,2048]{1,0:T(8,128)(2,1)S(1)} %copy-done), kind=kOutput, calls=%fused_computation.2 | convolution fusion | flops 12890800128 | bytes 28053504 | tf_op jit(solution)/shard_map/dot_general | solution.py:172
  503.3 1.2 copy.22
  (3 shorter events, 0.0 us)
Async XLA Ops:
  7.2 2.4 copy-start
  7.2 265.2 %reduce-scatter.2.cloned.1.call-start = ((), (), s32[]{:S(2)}) async-start(), calls=%async_computation.3 | async-start | bytes 25952256 | tf_op jit(solution)/shard_map/reduce_scatter | solution.py:171
  26.5 4.4 copy-start.2
  26.5 455.3 %all-gather.2.cloned.1.call-start = ((), (), s32[]{:S(2)}) async-start(), calls=%async_computation.2 | async-start | bytes 25952256 | tf_op jit(solution)/shard_map/all_gather | solution.py:156
  281.0 125.3 %copy-start.1 = (bf16[1024,768]{1,0:T(8,128)(2,1)S(1)}, bf16[1024,768]{1,0:T(8,128)(2,1)}, u32[]{:S(2)}) copy-start(bf16[1024,768]{1,0:T(8,128)(2,1)} %param.17) | copy-start | bytes 4718596
Sparse Core Ops, SparseCore 0:
  26.6 245.7 reduce-scatter.1
  275.9 205.8 all-gather.1

commit v2 on v0

v2 whole, which is shorter than its diff:
```python
import jax
import jax.numpy as jnp
from jax import lax
from jax.sharding import PartitionSpec as P
from jax.experimental import pallas as pl

LOSS_SCALE = 64.0
BETA_ONE = 0.9
BETA_TWO = 0.95
LEARN_RATE = 0.002
DECAY = 0.1
EPSILON = 1e-08
STEP_COUNT = 20.0
AXES = ("expert", "opt")


def rows_kernel(master_ref, rows_ref):
    experts = master_ref.shape[0]
    width = rows_ref.shape[1]
    for part in range(rows_ref.shape[0] // experts):
        rows_ref[part * experts : (part + 1) * experts, :] = master_ref[
            :, part * width : (part + 1) * width
        ].astype(rows_ref.dtype)


def expert_rows(master, model_width, per_step):
    experts, flat = master.shape
    steps = flat // model_width // per_step
    return pl.pallas_call(
        rows_kernel,
        grid=(steps,),
        in_specs=[pl.BlockSpec((experts, per_step * model_width), lambda i: (0, i))],
        out_specs=pl.BlockSpec((per_step * experts, model_width), lambda i: (i, 0)),
        out_shape=jax.ShapeDtypeStruct((flat // model_width * experts, model_width), jnp.bfloat16),
    )(master)


def adamw_kernel(grad_ref, master_ref, one_ref, two_ref, master_out, one_out, two_out, rows_out):
    experts = master_ref.shape[0]
    width = grad_ref.shape[1]
    for part in range(grad_ref.shape[0] // experts):
        rows = slice(part * experts, (part + 1) * experts)
        columns = slice(part * width, (part + 1) * width)
        gradient = grad_ref[rows, :].astype(jnp.float32)
        new_one = BETA_ONE * one_ref[:, columns] + (1.0 - BETA_ONE) * gradient
        new_two = BETA_TWO * two_ref[:, columns] + (1.0 - BETA_TWO) * gradient * gradient
        first_hat = new_one / (1.0 - BETA_ONE**STEP_COUNT)
        second_hat = new_two / (1.0 - BETA_TWO**STEP_COUNT)
        master = master_ref[:, columns]
        new_master = master - LEARN_RATE * (
            first_hat / (jnp.sqrt(second_hat) + EPSILON) + DECAY * master
        )
        one_out[:, columns] = new_one
        two_out[:, columns] = new_two
        master_out[:, columns] = new_master
        rows_out[rows, :] = new_master.astype(rows_out.dtype)


def adamw(grad_rows, master, moment_one, moment_two, per_step):
    experts, flat = master.shape
    width = grad_rows.shape[1]
    steps = flat // width // per_step
    wide = pl.BlockSpec((experts, per_step * width), lambda i: (0, i))
    tall = pl.BlockSpec((per_step * experts, width), lambda i: (i, 0))
    state = jax.ShapeDtypeStruct(master.shape, jnp.float32)
    return pl.pallas_call(
        adamw_kernel,
        grid=(steps,),
        in_specs=[tall, wide, wide, wide],
        out_specs=[wide, wide, wide, tall],
        out_shape=[state, state, state, jax.ShapeDtypeStruct(grad_rows.shape, jnp.bfloat16)],
    )(grad_rows, master, moment_one, moment_two)


def exchange(blocks):
    return lax.all_to_all(blocks, AXES, split_axis=0, concat_axis=0, tiled=True)


def owner_choice(placement, experts, owned):
    expert_ids = jnp.arange(experts, dtype=jnp.int32)
    row_ids = jnp.arange(owned, dtype=jnp.int32)
    chosen = (placement[:, None] == expert_ids[None, :])[:, None, None, :] & (
        row_ids[:, None] == row_ids[None, :]
    )[None, :, :, None]
    return chosen.reshape(placement.shape[0] * owned, owned * experts).astype(jnp.bfloat16)


def select(choice, rows):
    return jnp.dot(choice, rows, preferred_element_type=jnp.float32).astype(jnp.bfloat16)


def replica_weights(choice, rows, device_count):
    picked = select(choice, rows)
    width = picked.shape[1]
    return exchange(picked.reshape(device_count, -1, width)).reshape(-1, width)


def matmul_kernel(left_ref, right_ref, out_ref):
    out_ref[...] = jnp.dot(
        left_ref[...], right_ref[...], preferred_element_type=jnp.float32
    ).astype(out_ref.dtype)


def matmul(left, right, steps):
    rows, depth = left.shape
    width = right.shape[1]
    return pl.pallas_call(
        matmul_kernel,
        grid=(steps,),
        in_specs=[
            pl.BlockSpec((rows // steps, depth), lambda i: (i, 0)),
            pl.BlockSpec((depth, width), lambda i: (0, 0)),
        ],
        out_specs=pl.BlockSpec((rows // steps, width), lambda i: (i, 0)),
        out_shape=jax.ShapeDtypeStruct((rows, width), left.dtype),
    )(left, right)


def per_device(
    out_grad, saved_input, route, place_now, place_next, master, moment_one, moment_two, fwd_input
):
    device_count = lax.axis_size("expert") * lax.axis_size("opt")
    rows_here, model_width = out_grad.shape
    hidden_width = saved_input.shape[1]
    experts = master.shape[0]
    owned = hidden_width // device_count
    per_step = 4 if owned % 4 == 0 else 2
    capacity = 2 * rows_here // device_count
    slot_count = device_count * capacity
    target = route[:, 0]
    matches = (target[:, None] == jnp.arange(device_count, dtype=jnp.int32)[None, :]).astype(
        jnp.int32
    )
    earlier = jnp.sum(jnp.cumsum(matches, axis=0) * matches, axis=1) - 1
    position = target * capacity + earlier
    slots = (
        jnp.arange(slot_count, dtype=jnp.int32)[:, None] == position[None, :]
    ).astype(jnp.bfloat16)
    hidden_got = exchange(
        select(slots, saved_input).reshape(device_count, capacity, hidden_width)
    ).reshape(slot_count, hidden_width)
    grad_got = exchange(
        select(slots, out_grad).reshape(device_count, capacity, model_width)
    ).reshape(slot_count, model_width)
    partial = (
        lax.dot_general(
            hidden_got, grad_got, (((0,), (0,)), ((), ())), preferred_element_type=jnp.float32
        )
        / LOSS_SCALE
    ).astype(jnp.bfloat16)
    arrived = exchange(partial.reshape(device_count, owned, model_width)).reshape(
        hidden_width, model_width
    )
    choice_now = owner_choice(place_now, experts, owned)
    grad_rows = lax.dot_general(
        choice_now, arrived, (((0,), (0,)), ((), ())), preferred_element_type=jnp.float32
    )
    weight_now = replica_weights(
        choice_now, expert_rows(master, model_width, per_step), device_count
    )
    input_part = lax.dot_general(
        grad_got, weight_now, (((1,), (1,)), ((), ())), preferred_element_type=jnp.float32
    ).astype(jnp.bfloat16)
    returned = exchange(input_part.reshape(device_count, capacity, hidden_width)).reshape(
        slot_count, hidden_width
    )
    input_grad = lax.dot_general(
        slots, returned, (((0,), (0,)), ((), ())), preferred_element_type=jnp.float32
    ).astype(jnp.bfloat16)
    new_master, new_one, new_two, next_rows = adamw(
        grad_rows, master, moment_one, moment_two, per_step
    )
    weight_next = replica_weights(
        owner_choice(place_next, experts, owned), next_rows, device_count
    )
    fwd_output = matmul(fwd_input, weight_next, 4)
    return (input_grad, new_master, new_one, new_two, fwd_output)


def solution(mesh):
    return jax.shard_map(
        per_device,
        mesh=mesh,
        in_specs=(
            P(("expert", "opt"), None),
            P(("expert", "opt"), None),
            P(("expert", "opt"), None),
            P(),
            P(),
            P(None, ("expert", "opt")),
            P(None, ("expert", "opt")),
            P(None, ("expert", "opt")),
            P(("expert", "opt"), None),
        ),
        out_specs=(
            P(("expert", "opt"), None),
            P(None, ("expert", "opt")),
            P(None, ("expert", "opt")),
            P(None, ("expert", "opt")),
            P(("expert", "opt"), None),
        ),
        check_vma=False,
    )
```

time: 552 us -> 429 us (0.78); the launches traced: 542 us -> 428 us
  waiting for transfers between devices: 174 us -> 331 us
  local copies, waits for them, and re-layouts: 127 us -> 5.15 us
  blocking collectives: 97.4 us -> 0 us
  other arithmetic: 85.7 us -> 5.38 us
  Pallas kernels: 0 us -> 18.2 us
  matrix products: 30.9 us -> 38.2 us
    all_to_all x5 -> x6, waiting for transfers between devices: 174 us -> 331 us  [exchange(): return lax.all_to_all(blocks, AXES, split_axis=0, concat_axis=0, tiled=True)]
    all_to_all x1 -> x0, blocking collectives: 97.4 us -> none  [per_device(): lax.all_to_all(grad_send, ('expert', 'opt'), split_axis=0, concat_axis=0,...]
    unnamed x15 -> x6, local copies, waits for them, and re-layouts: 81.4 us -> 0.02 us
    all_to_all x7 -> x0, other arithmetic: 80 us -> none  [the longest x6 59.3 us: replica_weights(): lax.all_to_all(picked, ('expert', 'opt'), split_axis=0, concat_axis=0, ti...]
    pallas_call x0 -> x3, Pallas kernels: none -> 18.2 us  [the longest x1 7.28 us: matmul(): pl.pallas_call(matmul_kernel, grid=(steps,), in_specs=[pl.BlockSpec((rows...]
    all_to_all x2 -> x0, local copies, waits for them, and re-layouts: 12.9 us -> none  [per_device(): lax.all_to_all(pieces, ('expert', 'opt'), split_axis=0, concat_axis=0, ti...]
    scatter x2 -> x0, local copies, waits for them, and re-layouts: 11.7 us -> none  [the longest x1 7.3 us: per_device(): jnp.zeros((slot_count, model_width), jnp.bfloat16).at[position]]
    gather x3 -> x0, local copies, waits for them, and re-layouts: 11.3 us -> none  [the longest x2 8.62 us: replica_weights(): picked = jnp.take(weights.astype(jnp.bfloat16), placement, axis=0)]
  transfers between devices with their start and end apart: 5 -> 6, of which waited for: 4 -> 6; matrix products, arithmetic and copies ran while one was open for 25% -> 10% of each run, Pallas kernels for 0% -> 3%
where the time goes in v2:
time: 429 us; the launch traced here: 428 us
  waiting for transfers between devices  331 us (77%)
  matrix products  38.2 us (9%)
  starting transfers between devices  29.6 us (7%)
  Pallas kernels  18.2 us (4%)
  other arithmetic  5.38 us (1%)
  local copies, waits for them, and re-layouts  5.15 us (1%)
    all_to_all x6, waiting for transfers between devices, exchange(): return lax.all_to_all(blocks, AXES, split_axis=0, concat_axis=0, tiled=True)  331 us
    all_to_all x6, starting transfers between devices, exchange(): return lax.all_to_all(blocks, AXES, split_axis=0, concat_axis=0, tiled=True)  29.6 us
    dot_general x4, matrix products, select(): jnp.dot(choice, rows, preferred_element_type=jnp.float32)  15.4 us
  transfers between devices with their start and end apart: 6, of which 6 were waited for; matrix products, arithmetic and copies ran while one was open for 10% of the time, Pallas kernels for 3%

profile of v2, /device:TPU:0, one launch (start us, length us, event | category | flops | bytes accessed | tf_op | source)
XLA Modules:
  0.0 428.4 jit_solution(15179374402074965343)
XLA Ops:
  0.6 0.0 copy-start
  0.6 0.8 fusion.10
  1.5 1.2 reduce-window.6
  2.6 0.2 slice_reduce_fusion
  2.9 0.8 fusion.9
  3.7 0.7 add_add_fusion
  4.4 3.3 fusion.3
  7.7 7.4 %all-to-all-start.3 = ((bf16[32,32,768]{2,1,0:T(8,128)(2,1)}), bf16[32,32,768]{2,1,0:T(8,128)(2,1)}, u32[]{:S(2)}, u32[]{:S(2)}) async-start(bf16[32,32,768]{2,1,0:T(8,128)(2,1)} %bitcast.58), calls=%async_computation.3 | async-start | bytes 3145728 | tf_op jit(solution)/shard_map/all_to_all | solution.py:76
  15.1 0.0 copy-done
  15.1 4.3 %convolution_convert_fusion = bf16[1024,2048]{1,0:T(8,128)(2,1)} fusion(bf16[512,2048]{1,0:T(8,128)(2,1)S(1)} %copy-done, s32[512]{0:T(512)S(1)} %add_add_fusion), kind=kOutput, calls=%fused_computation.2 | convolution fusion | flops 2150105088 | bytes 6293504 | tf_op jit(solution)/shard_map/dot_general | solution.py:89
  19.5 33.1 %all-to-all-done.3 = bf16[32,32,768]{2,1,0:T(8,128)(2,1)} async-done(((bf16[32,32,768]{2,1,0:T(8,128)(2,1)}), bf16[32,32,768]{2,1,0:T(8,128)(2,1)}, u32[]{:S(2)}, u32[]{:S(2)}) %all-to-all-start.3) | async-done | bytes 1572896 | tf_op jit(solution)/shard_map/all_to_all | solution.py:76
  52.6 0.0 copy-start.1
  52.6 0.0 copy-start.2
  52.6 3.8 all-to-all-start
  56.3 0.0 copy-done.1
  56.4 0.0 copy-done.2
  56.4 1.9 broadcast_and_fusion
  58.2 2.9 and.44
  61.2 4.3 %shard_map.128 = bf16[192,2048]{1,0:T(8,128)(2,1)} custom-call(f32[8,49152]{1,0:T(8,128)} %master_ref.3), custom_call_target="tpu_custom_call" | custom-call | tf_op jit(solution)/shard_map/pallas_call | solution.py:29
  65.5 3.9 convolution_convert_fusion.2
  69.4 81.2 %all-to-all-done = bf16[32,32,2048]{2,1,0:T(8,128)(2,1)} async-done(((bf16[32,32,2048]{2,1,0:T(8,128)(2,1)}), bf16[32,32,2048]{2,1,0:T(8,128)(2,1)}, u32[]{:S(2)}, u32[]{:S(2)}) %all-to-all-start) | async-done | bytes 4194336 | tf_op jit(solution)/shard_map/all_to_all | solution.py:76
  150.6 5.2 %all-to-all-start.1 = ((bf16[32,24,2048]{2,1,0:T(8,128)(2,1)}), bf16[32,24,2048]{2,1,0:T(8,128)(2,1)}, u32[]{:S(2)}, u32[]{:S(2)}) async-start(bf16[32,24,2048]{2,1,0:T(8,128)(2,1)} %bitcast.54), calls=%async_computation.1 | async-start | bytes 6291456 | tf_op jit(solution)/shard_map/all_to_all | solution.py:76
  155.7 7.8 %fusion = bf16[768,2048]{1,0:T(8,128)(2,1)} fusion(bf16[32,32,768]{2,1,0:T(8,128)(2,1)} %all-to-all-done.3, bf16[32,32,2048]{2,1,0:T(8,128)(2,1)} %all-to-all-done), kind=kOutput, calls=%fused_computation.1 | convolution fusion | flops 3224371200 | bytes 8912896 | tf_op jit(solution)/shard_map/dot_general | solution.py:146
  163.5 63.8 %all-to-all-done.1 = bf16[32,24,2048]{2,1,0:T(8,128)(2,1)} async-done(((bf16[32,24,2048]{2,1,0:T(8,128)(2,1)}), bf16[32,24,2048]{2,1,0:T(8,128)(2,1)}, u32[]{:S(2)}, u32[]{:S(2)}) %all-to-all-start.1) | async-done | bytes 3145760 | tf_op jit(solution)/shard_map/all_to_all | solution.py:76
  227.3 4.9 %all-to-all-start.4 = ((bf16[32,24,2048]{2,1,0:T(8,128)(2,1)}), bf16[32,24,2048]{2,1,0:T(8,128)(2,1)}, u32[]{:S(2)}, u32[]{:S(2)}) async-start(bf16[32,24,2048]{2,1,0:T(8,128)(2,1)} %bitcast.56), calls=%async_computation.4 | async-start | bytes 6291456 | tf_op jit(solution)/shard_map/all_to_all | solution.py:76
  232.2 7.8 %convolution_convert_fusion.3 = bf16[1024,768]{1,0:T(8,128)(2,1)} fusion(bf16[1024,2048]{1,0:T(8,128)(2,1)} %bitcast.4, bf16[768,2048]{1,0:T(8,128)(2,1)} %bitcast.6), kind=kOutput, calls=%fused_computation.9 | convolution fusion | flops 3222011904 | bytes 8912896 | tf_op jit(solution)/shard_map/dot_general | solution.py:161
  240.0 63.7 %all-to-all-done.4 = bf16[32,24,2048]{2,1,0:T(8,128)(2,1)} async-done(((bf16[32,24,2048]{2,1,0:T(8,128)(2,1)}), bf16[32,24,2048]{2,1,0:T(8,128)(2,1)}, u32[]{:S(2)}, u32[]{:S(2)}) %all-to-all-start.4) | async-done | bytes 3145760 | tf_op jit(solution)/shard_map/all_to_all | solution.py:76
  303.6 4.7 %all-to-all-start.2 = ((bf16[32,32,768]{2,1,0:T(8,128)(2,1)}), bf16[32,32,768]{2,1,0:T(8,128)(2,1)}, u32[]{:S(2)}, u32[]{:S(2)}) async-start(bf16[32,32,768]{2,1,0:T(8,128)(2,1)} %bitcast.57), calls=%async_computation.2 | async-start | bytes 3145728 | tf_op jit(solution)/shard_map/all_to_all | solution.py:76
  308.3 2.0 and.47
  310.3 3.8 fusion.11.grad_ref
  314.1 6.6 %shard_map.129 = (f32[8,49152]{1,0:T(8,128)}, f32[8,49152]{1,0:T(8,128)}, f32[8,49152]{1,0:T(8,128)}, bf16[192,2048]{1,0:T(8,128)(2,1)}) custom-call(f32[192,2048]{1,0:T(8,128)} %fusion.11.grad_ref, f32[8,49152]{1,0:T(8,128)} %master_ref.3, f32[8,49152]{1,0:T(8,128)} %one_ref.1, f32[8,49152]{1,0:T(8,128)} %two_ref.1), custom_call_target="tpu_custom_call" | custom-call | tf_op jit(solution)/shard_map/pallas_call | solution.py:66
  320.7 3.8 convolution_convert_fusion.1
  324.5 21.2 %all-to-all-done.2 = bf16[32,32,768]{2,1,0:T(8,128)(2,1)} async-done(((bf16[32,32,768]{2,1,0:T(8,128)(2,1)}), bf16[32,32,768]{2,1,0:T(8,128)(2,1)}, u32[]{:S(2)}, u32[]{:S(2)}) %all-to-all-start.2) | async-done | bytes 1572896 | tf_op jit(solution)/shard_map/all_to_all | solution.py:76
  345.7 3.7 all-to-all-start.5
  349.5 3.5 fusion.4
  353.0 68.1 %all-to-all-done.5 = bf16[32,24,2048]{2,1,0:T(8,128)(2,1)} async-done(((bf16[32,24,2048]{2,1,0:T(8,128)(2,1)}), bf16[32,24,2048]{2,1,0:T(8,128)(2,1)}, u32[]{:S(2)}, u32[]{:S(2)}) %all-to-all-start.5) | async-done | bytes 3145760 | tf_op jit(solution)/shard_map/all_to_all | solution.py:76
  421.1 7.3 %shard_map.130 = bf16[1024,2048]{1,0:T(8,128)(2,1)} custom-call(bf16[1024,768]{1,0:T(8,128)(2,1)} %left_ref.1, bf16[768,2048]{1,0:T(8,128)(2,1)} %bitcast.14.right_ref), custom_call_target="tpu_custom_call" | custom-call | tf_op jit(solution)/shard_map/pallas_call | solution.py:107
  (4 shorter events, 0.1 us)
Async XLA Ops:
  0.6 14.5 %copy-start = (bf16[512,2048]{1,0:T(8,128)(2,1)S(1)}, bf16[512,2048]{1,0:T(8,128)(2,1)}, u32[]{:S(2)}) copy-start(bf16[512,2048]{1,0:T(8,128)(2,1)} %param.9) | copy-start | bytes 6291460
  7.7 44.9 %all-to-all-start.3 = ((bf16[32,32,768]{2,1,0:T(8,128)(2,1)}), bf16[32,32,768]{2,1,0:T(8,128)(2,1)}, u32[]{:S(2)}, u32[]{:S(2)}) async-start(bf16[32,32,768]{2,1,0:T(8,128)(2,1)} %bitcast.58), calls=%async_computation.3 | async-start | bytes 3145728 | tf_op jit(solution)/shard_map/all_to_all | solution.py:76
  52.6 3.8 copy-start.1
  52.6 3.8 copy-start.2
  52.6 98.0 %all-to-all-start = ((bf16[32,32,2048]{2,1,0:T(8,128)(2,1)}), bf16[32,32,2048]{2,1,0:T(8,128)(2,1)}, u32[]{:S(2)}, u32[]{:S(2)}) async-start(bf16[32,32,2048]{2,1,0:T(8,128)(2,1)} %bitcast.55), calls=%async_computation | async-start | bytes 8388608 | tf_op jit(solution)/shard_map/all_to_all | solution.py:76
  150.6 76.8 %all-to-all-start.1 = ((bf16[32,24,2048]{2,1,0:T(8,128)(2,1)}), bf16[32,24,2048]{2,1,0:T(8,128)(2,1)}, u32[]{:S(2)}, u32[]{:S(2)}) async-start(bf16[32,24,2048]{2,1,0:T(8,128)(2,1)} %bitcast.54), calls=%async_computation.1 | async-start | bytes 6291456 | tf_op jit(solution)/shard_map/all_to_all | solution.py:76
  227.3 76.3 %all-to-all-start.4 = ((bf16[32,24,2048]{2,1,0:T(8,128)(2,1)}), bf16[32,24,2048]{2,1,0:T(8,128)(2,1)}, u32[]{:S(2)}, u32[]{:S(2)}) async-start(bf16[32,24,2048]{2,1,0:T(8,128)(2,1)} %bitcast.56), calls=%async_computation.4 | async-start | bytes 6291456 | tf_op jit(solution)/shard_map/all_to_all | solution.py:76
  303.6 42.1 %all-to-all-start.2 = ((bf16[32,32,768]{2,1,0:T(8,128)(2,1)}), bf16[32,32,768]{2,1,0:T(8,128)(2,1)}, u32[]{:S(2)}, u32[]{:S(2)}) async-start(bf16[32,32,768]{2,1,0:T(8,128)(2,1)} %bitcast.57), calls=%async_computation.2 | async-start | bytes 3145728 | tf_op jit(solution)/shard_map/all_to_all | solution.py:76
  345.7 75.3 %all-to-all-start.5 = ((bf16[32,24,2048]{2,1,0:T(8,128)(2,1)}), bf16[32,24,2048]{2,1,0:T(8,128)(2,1)}, u32[]{:S(2)}, u32[]{:S(2)}) async-start(bf16[32,24,2048]{2,1,0:T(8,128)(2,1)} %bitcast.53), calls=%async_computation.5 | async-start | bytes 6291456 | tf_op jit(solution)/shard_map/all_to_all | solution.py:76

commit v3 on v2

--- a/solution.py
+++ b/solution.py
@@ -1,8 +1,11 @@
+import functools
+
 import jax
 import jax.numpy as jnp
 from jax import lax
 from jax.sharding import PartitionSpec as P
 from jax.experimental import pallas as pl
+from jax.experimental.pallas import tpu as pltpu
 
 LOSS_SCALE = 64.0
 BETA_ONE = 0.9
@@ -76,6 +79,78 @@
     return lax.all_to_all(blocks, AXES, split_axis=0, concat_axis=0, tiled=True)
 
 
+def exchange_kernel(count, members, *refs):
+    device_count = refs[0].shape[0]
+    sources, targets = refs[:count], refs[count : 2 * count]
+    send_sem, recv_sem, own_sem = refs[2 * count :]
+    me = lax.axis_index("expert") * members + lax.axis_index("opt")
+    barrier = pltpu.get_barrier_semaphore()
+
+    def coordinates(step):
+        other = lax.rem(me + step, device_count)
+        return other, (other // members, lax.rem(other, members))
+
+    def greet(step, carry):
+        pl.semaphore_signal(
+            barrier,
+            inc=1,
+            device_id=coordinates(step)[1],
+            device_id_type=pl.DeviceIdType.MESH,
+        )
+        return carry
+
+    lax.fori_loop(1, device_count, greet, 0)
+    pl.semaphore_wait(barrier, device_count - 1)
+    own = [
+        pltpu.make_async_copy(sources[k].at[me], targets[k].at[me], own_sem.at[k])
+        for k in range(count)
+    ]
+
+    def copy(k, step):
+        other, place = coordinates(step)
+        return pltpu.make_async_remote_copy(
+            src_ref=sources[k].at[other],
+            dst_ref=targets[k].at[me],
+            send_sem=send_sem.at[k, step],
+            recv_sem=recv_sem.at[k, step],
+            device_id=place,
+            device_id_type=pl.DeviceIdType.MESH,
+        )
+
+    def start(step, carry):
+        for k in range(count):
+            copy(k, step).start()
+        return carry
+
+    def finish(step, carry):
+        for k in range(count):
+            copy(k, step).wait()
+        return carry
+
+    lax.fori_loop(1, device_count, start, 0)
+    for piece in own:
+        piece.start()
+    for piece in own:
+        piece.wait()
+    lax.fori_loop(1, device_count, finish, 0)
+
+
+def exchange_together(*blocks):
+    count, device_count = len(blocks), blocks[0].shape[0]
+    return pl.pallas_call(
+        functools.partial(exchange_kernel, count, lax.axis_size("opt")),
+        in_specs=[pl.BlockSpec(memory_space=pl.ANY)] * count,
+        out_specs=[pl.BlockSpec(memory_space=pl.ANY)] * count,
+        out_shape=[jax.ShapeDtypeStruct(block.shape, block.dtype) for block in blocks],
+        scratch_shapes=[
+            pltpu.SemaphoreType.DMA((count, device_count)),
+            pltpu.SemaphoreType.DMA((count, device_count)),
+            pltpu.SemaphoreType.DMA((count,)),
+        ],
+        compiler_params=pltpu.CompilerParams(collective_id=0, has_side_effects=True),
+    )(*blocks)
+
+
 def owner_choice(placement, experts, owned):
     expert_ids = jnp.arange(experts, dtype=jnp.int32)
     row_ids = jnp.arange(owned, dtype=jnp.int32)
@@ -136,12 +211,16 @@
     slots = (
         jnp.arange(slot_count, dtype=jnp.int32)[:, None] == position[None, :]
     ).astype(jnp.bfloat16)
-    hidden_got = exchange(
-        select(slots, saved_input).reshape(device_count, capacity, hidden_width)
-    ).reshape(slot_count, hidden_width)
-    grad_got = exchange(
-        select(slots, out_grad).reshape(device_count, capacity, model_width)
-    ).reshape(slot_count, model_width)
+    choice_now = owner_choice(place_now, experts, owned)
+    picked_now = select(choice_now, expert_rows(master, model_width, per_step))
+    hidden_got, grad_got, weight_now = exchange_together(
+        select(slots, saved_input).reshape(device_count, capacity, hidden_width),
+        select(slots, out_grad).reshape(device_count, capacity, model_width),
+        picked_now.reshape(device_count, owned, model_width),
+    )
+    hidden_got = hidden_got.reshape(slot_count, hidden_width)
+    grad_got = grad_got.reshape(slot_count, model_width)
+    weight_now = weight_now.reshape(hidden_width, model_width)
     partial = (
         lax.dot_general(
             hidden_got, grad_got, (((0,), (0,)), ((), ())), preferred_element_type=jnp.float32
@@ -151,12 +230,8 @@
     arrived = exchange(partial.reshape(device_count, owned, model_width)).reshape(
         hidden_width, model_width
     )
-    choice_now = owner_choice(place_now, experts, owned)
     grad_rows = lax.dot_general(
         choice_now, arrived, (((0,), (0,)), ((), ())), preferred_element_type=jnp.float32
-    )
-    weight_now = replica_weights(
-        choice_now, expert_rows(master, model_width, per_step), device_count
     )
     input_part = lax.dot_general(
         grad_got, weight_now, (((1,), (1,)), ((), ())), preferred_element_type=jnp.float32

time: 429 us -> 475 us (1.11)
  Pallas kernels: 18.2 us -> 205 us
  waiting for transfers between devices: 331 us -> 153 us
  starting transfers between devices: 29.6 us -> 67.1 us
    pallas_call x0 -> x1, Pallas kernels: none -> 187 us  [exchange_together(): pl.pallas_call(functools.partial(exchange_kernel, count, lax.axis_size('o...]
    all_to_all x6 -> x3, waiting for transfers between devices: 331 us -> 153 us  [exchange(): return lax.all_to_all(blocks, AXES, split_axis=0, concat_axis=0, tiled=True)]
    all_to_all x6 -> x3, starting transfers between devices: 29.6 us -> 67.1 us  [exchange(): return lax.all_to_all(blocks, AXES, split_axis=0, concat_axis=0, tiled=True)]
  transfers between devices with their start and end apart: 6 -> 3, of which waited for: 6 -> 3; matrix products, arithmetic and copies ran while one was open for 10% -> 4% of each run, Pallas kernels for 3% -> 1%
where the time goes in v3:
time: 475 us; the launch traced here: 474 us
  Pallas kernels  205 us (43%)
  waiting for transfers between devices  153 us (32%)
  starting transfers between devices  67.1 us (14%)
  matrix products  37.1 us (8%)
  other arithmetic  6.05 us (1%)
  local copies, waits for them, and re-layouts  5.14 us (1%)
    pallas_call x1, Pallas kernels, exchange_together(): pl.pallas_call(functools.partial(exchange_kernel, count, lax.axis_size('o...  187 us
    all_to_all x3, waiting for transfers between devices, exchange(): return lax.all_to_all(blocks, AXES, split_axis=0, concat_axis=0, tiled=True)  153 us
    all_to_all x3, starting transfers between devices, exchange(): return lax.all_to_all(blocks, AXES, split_axis=0, concat_axis=0, tiled=True)  67.1 us
    dot_general x4, matrix products, select(): jnp.dot(choice, rows, preferred_element_type=jnp.float32)  14.2 us
  transfers between devices with their start and end apart: 3, of which 3 were waited for; matrix products, arithmetic and copies ran while one was open for 4% of the time, Pallas kernels for 1%

profile of v3, /device:TPU:0, one launch (start us, length us, event | category | flops | bytes accessed | tf_op | source)
XLA Modules:
  0.0 474.0 jit_solution(5495955107357182633)
XLA Ops:
  0.6 0.0 copy-start
  0.7 0.8 fusion.10
  1.5 1.2 reduce-window.6
  2.7 0.2 slice_reduce_fusion
  2.9 0.8 fusion.9
  3.7 0.7 add_add_fusion
  4.4 4.3 shard_map.128
  8.7 0.7 iota_compare_fusion.11
  9.4 1.9 broadcast_and_fusion
  11.3 2.9 and.44
  14.2 3.3 fusion.3
  17.5 0.0 copy-done
  17.5 0.0 copy-start.1
  17.5 4.3 convolution_convert_fusion
  21.9 0.0 copy-done.1
  21.9 2.8 convolution_convert_fusion.2
  24.6 186.8 %shard_map.129 = (bf16[32,32,768]{2,1,0:T(8,128)(2,1)}, bf16[32,32,2048]{2,1,0:T(8,128)(2,1)}, bf16[32,24,2048]{2,1,0:T(8,128)(2,1)}) custom-call(bf16[32,32,768]{2,1,0:T(8,128)(2,1)} %bitcast.58, bf16[32,32,2048]{2,1,0:T(8,128)(2,1)} %bitcast.55, bf16[32,24,2048]{2,1,0:T(8,128)(2,1)} %bitcast.54), custom_call_target="tpu_custom_call" | custom-call | tf_op jit(solution)/shard_map/pallas_call | solution.py:140
  211.4 7.8 %fusion = bf16[768,2048]{1,0:T(8,128)(2,1)} fusion(bf16[32,32,768]{2,1,0:T(8,128)(2,1)} %get-tuple-element.14, bf16[32,32,2048]{2,1,0:T(8,128)(2,1)} %get-tuple-element.12), kind=kOutput, calls=%fused_computation.1 | convolution fusion | flops 3224371200 | bytes 8912896 | tf_op jit(solution)/shard_map/dot_general | solution.py:225
  219.2 58.7 %all-to-all-start.1 = ((bf16[32,24,2048]{2,1,0:T(8,128)(2,1)}), bf16[32,24,2048]{2,1,0:T(8,128)(2,1)}, u32[]{:S(2)}, u32[]{:S(2)}) async-start(bf16[32,24,2048]{2,1,0:T(8,128)(2,1)} %bitcast.56), calls=%async_computation.1 | async-start | bytes 6291456 | tf_op jit(solution)/shard_map/all_to_all | solution.py:79
  277.9 7.8 %convolution_convert_fusion.3 = bf16[1024,768]{1,0:T(8,128)(2,1)} fusion(bf16[1024,2048]{1,0:T(8,128)(2,1)} %bitcast.62, bf16[768,2048]{1,0:T(8,128)(2,1)} %bitcast.63), kind=kOutput, calls=%fused_computation.9 | convolution fusion | flops 3222011904 | bytes 8912896 | tf_op jit(solution)/shard_map/dot_general | solution.py:236
  285.7 63.6 %all-to-all-done.1 = bf16[32,24,2048]{2,1,0:T(8,128)(2,1)} async-done(((bf16[32,24,2048]{2,1,0:T(8,128)(2,1)}), bf16[32,24,2048]{2,1,0:T(8,128)(2,1)}, u32[]{:S(2)}, u32[]{:S(2)}) %all-to-all-start.1) | async-done | bytes 3145760 | tf_op jit(solution)/shard_map/all_to_all | solution.py:79
  349.3 4.7 all-to-all-start
  354.0 2.0 and.47
  355.9 3.8 fusion.11.grad_ref
  359.8 6.6 %shard_map.130 = (f32[8,49152]{1,0:T(8,128)}, f32[8,49152]{1,0:T(8,128)}, f32[8,49152]{1,0:T(8,128)}, bf16[192,2048]{1,0:T(8,128)(2,1)}) custom-call(f32[192,2048]{1,0:T(8,128)} %fusion.11.grad_ref, f32[8,49152]{1,0:T(8,128)} %master_ref.3, f32[8,49152]{1,0:T(8,128)} %one_ref.1, f32[8,49152]{1,0:T(8,128)} %two_ref.1), custom_call_target="tpu_custom_call" | custom-call | tf_op jit(solution)/shard_map/pallas_call | solution.py:69
  366.3 3.8 convolution_convert_fusion.1
  370.2 21.2 %all-to-all-done = bf16[32,32,768]{2,1,0:T(8,128)(2,1)} async-done(((bf16[32,32,768]{2,1,0:T(8,128)(2,1)}), bf16[32,32,768]{2,1,0:T(8,128)(2,1)}, u32[]{:S(2)}, u32[]{:S(2)}) %all-to-all-start) | async-done | bytes 1572896 | tf_op jit(solution)/shard_map/all_to_all | solution.py:79
  391.4 3.7 all-to-all-start.2
  395.2 3.5 fusion.4
  398.7 68.1 %all-to-all-done.2 = bf16[32,24,2048]{2,1,0:T(8,128)(2,1)} async-done(((bf16[32,24,2048]{2,1,0:T(8,128)(2,1)}), bf16[32,24,2048]{2,1,0:T(8,128)(2,1)}, u32[]{:S(2)}, u32[]{:S(2)}) %all-to-all-start.2) | async-done | bytes 3145760 | tf_op jit(solution)/shard_map/all_to_all | solution.py:79
  466.8 7.3 %shard_map.131 = bf16[1024,2048]{1,0:T(8,128)(2,1)} custom-call(bf16[1024,768]{1,0:T(8,128)(2,1)} %left_ref.1, bf16[768,2048]{1,0:T(8,128)(2,1)} %bitcast.14.right_ref), custom_call_target="tpu_custom_call" | custom-call | tf_op jit(solution)/shard_map/pallas_call | solution.py:182
  (3 shorter events, 0.0 us)
Async XLA Ops:
  0.6 16.9 %copy-start = (bf16[512,2048]{1,0:T(8,128)(2,1)S(1)}, bf16[512,2048]{1,0:T(8,128)(2,1)}, u32[]{:S(2)}) copy-start(bf16[512,2048]{1,0:T(8,128)(2,1)} %param.9) | copy-start | bytes 6291460
  17.5 4.4 copy-start.1
  219.2 130.1 %all-to-all-start.1 = ((bf16[32,24,2048]{2,1,0:T(8,128)(2,1)}), bf16[32,24,2048]{2,1,0:T(8,128)(2,1)}, u32[]{:S(2)}, u32[]{:S(2)}) async-start(bf16[32,24,2048]{2,1,0:T(8,128)(2,1)} %bitcast.56), calls=%async_computation.1 | async-start | bytes 6291456 | tf_op jit(solution)/shard_map/all_to_all | solution.py:79
  349.3 42.1 %all-to-all-start = ((bf16[32,32,768]{2,1,0:T(8,128)(2,1)}), bf16[32,32,768]{2,1,0:T(8,128)(2,1)}, u32[]{:S(2)}, u32[]{:S(2)}) async-start(bf16[32,32,768]{2,1,0:T(8,128)(2,1)} %bitcast.57), calls=%async_computation | async-start | bytes 3145728 | tf_op jit(solution)/shard_map/all_to_all | solution.py:79
  391.4 75.3 %all-to-all-start.2 = ((bf16[32,24,2048]{2,1,0:T(8,128)(2,1)}), bf16[32,24,2048]{2,1,0:T(8,128)(2,1)}, u32[]{:S(2)}, u32[]{:S(2)}) async-start(bf16[32,24,2048]{2,1,0:T(8,128)(2,1)} %bitcast.53), calls=%async_computation.2 | async-start | bytes 6291456 | tf_op jit(solution)/shard_map/all_to_all | solution.py:79
